TPU v7x, 256 devices: a whole 4x4x8 slice. The times are simulated.
256 devices in a mesh: blk: 16 (over z, x_hi), leaf: 8 (over y, core), rhs: 2 (over x_lo).
Axes of the slice: x: 4 (x_hi: 2, x_lo: 2; x = x_hi * 2 + x_lo), y: 4, z: 8, core: 2. Of those that a mesh axis runs over, the one named last changes fastest.
Arguments:
- residual: float32 [32, 8, 65536], P('rhs', 'leaf', 'blk'), may hold values from -160 to 160
- points: float32 [3, 8, 65536], P(None, 'leaf', 'blk'), may hold values from -12330 to 12330
- noise: float32 [8, 65536], P('leaf', 'blk'), may hold values from 1 to 2
- block_list: int32 [8, 8, 256], P('leaf'), may hold values from 0 to 1, as said below
Outputs:
- correction: float32 [32, 8, 65536], P('rhs', 'leaf', 'blk')
- new_residual: float32 [32, 8, 65536], P('rhs', 'leaf', 'blk')
- basis: float32 [128, 8, 65536], P('rhs', 'leaf', 'blk')
Inputs may be any that keep to these rules, and one draw needn't show every extreme that they name: The list is symmetric: block_list[t, k, i] == block_list[t, 7 - k, (i + d) mod 256] with d the offset of entry k.
All inputs are finite; a program needn't handle non-finite values.
Results may differ from a plain program's by a relative error of at most 0.007.
Values sent between devices are 32-bit elements; how exact they have to be, the bound alone decides.
A program may use at most 128 MiB of HBM per device.

v0:
```python
import jax
import jax.numpy as jnp
from jax import lax
from jax.sharding import PartitionSpec as P

M = 32
S = 4
BS = 256
REACH = 4
SUPPORT = 1408


centre_shift = 1.5
amplitude = 1.1
exact = lax.Precision.HIGHEST


def extended(x, sides, width):
    for axis, dim in sides:
        count, length = (lax.axis_size(axis), x.shape[dim])
        up = [(i, (i + 1) % count) for i in range(count)]
        down = [(j, i) for i, j in up]
        last = lax.slice_in_dim(x, length - width, length, axis=dim)
        leading = lax.slice_in_dim(x, 0, width, axis=dim)
        before = lax.ppermute(last, axis, up)
        after = lax.ppermute(leading, axis, down)
        x = jnp.concatenate([before, x, after], axis=dim)
    return x


def kernel_tile(near_points, own_points):
    squared = (near_points[0][:, None] - own_points[0][None, :]) ** 2
    squared = squared + (near_points[1][:, None] - own_points[1][None, :]) ** 2
    squared = squared + (near_points[2][:, None] - own_points[2][None, :]) ** 2
    radius = jnp.sqrt(squared) / SUPPORT
    remain = jnp.maximum(1.0 - radius, 0.0)
    return remain * remain * (remain * remain) * (4.0 * radius + 1.0) * (amplitude / SUPPORT)


def band_product(field_wide, points_wide, weights, rows_out):
    per_turn = rows_out // 8
    count = field_wide.shape[0]

    def turn(carry, index):
        pieces = []
        for inner in range(per_turn):
            block = index * per_turn + inner
            own_points = lax.dynamic_slice_in_dim(points_wide, (block + REACH) * BS, BS, 1)
            total = jnp.zeros((count, BS), jnp.float32)
            for offset in range(2 * REACH + 1):
                column_at = (block + offset) * BS
                near_points = lax.dynamic_slice_in_dim(points_wide, column_at, BS, 1)
                near_field = lax.dynamic_slice_in_dim(field_wide, column_at, BS, 1)
                listed = lax.dynamic_index_in_dim(weights[offset], block, 0, False)
                tile = kernel_tile(near_points, own_points) * listed
                total = total + jnp.dot(near_field, tile, precision=exact)
            pieces.append(total)
        return (carry, jnp.concatenate(pieces, axis=1))

    carry, parts = lax.scan(turn, jnp.zeros((), jnp.int32), jnp.arange(8, dtype=jnp.int32))
    return jnp.moveaxis(parts, 0, 1).reshape(count, rows_out * BS)


def galerkin(gram, count_points, count_sides):
    normed = gram / count_points
    basis_count = normed.shape[0] - count_sides
    gram_basis = normed[:basis_count, :basis_count]
    factor_low = jnp.linalg.cholesky(gram_basis)
    inverse_low = lax.linalg.triangular_solve(
        factor_low, jnp.eye(basis_count, dtype=jnp.float32), left_side=True, lower=True
    )
    cross = normed[:basis_count, count_sides:] + centre_shift * gram_basis
    projected = jnp.dot(
        jnp.dot(inverse_low, cross, precision=exact), inverse_low.T, precision=exact
    )
    projected = 0.5 * (projected + projected.T)
    small_side = jnp.dot(inverse_low, gram_basis[:, :count_sides], precision=exact)
    proj_factor = jnp.linalg.cholesky(projected)
    halfway = lax.linalg.triangular_solve(proj_factor, small_side, left_side=True, lower=True)
    coeffs = lax.linalg.triangular_solve(
        proj_factor, halfway, left_side=True, lower=True, transpose_a=True
    )
    combo = jnp.dot(coeffs.T, inverse_low, precision=exact)
    return (inverse_low, combo)


def row_products(rows):
    return lax.dot_general(rows, rows, (((1,), (1,)), ((), ())), precision=exact)


def local(residual, points, noise, block_list):
    field = residual[:, 0]
    coords = points[:, 0]
    nugget = noise[0]
    own_rows = field.shape[1]
    own_blocks = own_rows // BS
    first_block = lax.axis_index("blk") * own_blocks
    listed = block_list[0].astype(jnp.float32)
    nine = jnp.concatenate(
        [listed[:REACH], jnp.ones((1, listed.shape[1]), jnp.float32), listed[REACH:]], axis=0
    )
    margin = S * REACH
    wrapped = jnp.concatenate([nine[:, -margin:], nine, nine[:, :margin]], axis=1)
    powers = [field]
    rim = REACH * BS
    coords_wide = extended(coords, (("blk", 1),), rim)
    own_weights = lax.dynamic_slice_in_dim(wrapped, first_block + margin, own_blocks, 1)
    current = field
    for power_step in range(S):
        widened = extended(current, (("blk", 1),), rim)
        current = (
            band_product(widened, coords_wide, own_weights, own_blocks)
            + (nugget - centre_shift) * current
        )
        powers.append(current)
    half_panel = jnp.stack(powers, axis=0)
    count_points = own_rows * lax.axis_size("blk") * lax.axis_size("leaf")
    sides_here = field.shape[0]
    whole = lax.all_gather(half_panel, "rhs", axis=1, tiled=True)
    flat = whole.reshape(-1, own_rows)
    gram = lax.psum(row_products(flat), ("blk", "leaf"))
    inverse_low, combo = galerkin(gram, count_points, M)
    first_rows = flat[: S * M]
    image = flat[M:] + centre_shift * first_rows
    part = lax.axis_index("rhs")
    basis_here = S * M // lax.axis_size("rhs")
    mine_low = lax.dynamic_slice_in_dim(inverse_low, part * basis_here, basis_here, 0)
    mine_combo = lax.dynamic_slice_in_dim(combo, part * sides_here, sides_here, 0)
    correction = jnp.dot(mine_combo, first_rows, precision=exact)
    new_residual = field - jnp.dot(mine_combo, image, precision=exact)
    basis = jnp.dot(mine_low, first_rows, precision=exact)
    return (correction[:, None], new_residual[:, None], basis[:, None])


def solution(mesh):
    placed = (
        P("rhs", "leaf", "blk"),
        P(None, "leaf", "blk"),
        P("leaf", "blk"),
        P("leaf", None, None),
    )
    return jax.shard_map(
        local,
        mesh=mesh,
        in_specs=placed,
        out_specs=(P("rhs", "leaf", "blk"), P("rhs", "leaf", "blk"), P("rhs", "leaf", "blk")),
        check_vma=False,
    )
```

profile of v0, /device:TPU:16, one launch (start us, length us, event | category | flops | bytes accessed | tf_op | source)
XLA Modules:
  0.0 2104.2 jit_solution(17787421845742051918)
XLA Ops:
  8.1 3.1 collective-permute-start.2
  11.2 5.4 collective-permute-start.3
  17.8 5.6 collective-permute-start.1
  26.3 206.0 %while.52 = (s32[]{:T(128)}, f32[8,16,512]{2,1,0:T(8,128)S(1)}, s32[8]{0:T(128)S(1)}, f32[16,6144]{1,0:T(8,128)S(1)}, f32[3,6144]{1,0:T(4,128)S(1)}, /*index=5*/...) while((s32[]{:T(128)}, f32[8,16,512]{2,1,0:T(8,128)S(1)}, ...), condition=%wide.region_1.2_spmd, body=%wide.region_0.1_spmd.sunk | while | flops 246620224 | bytes 1092197 | solution.py:60
  232.8 5.6 collective-permute-start.5
  238.8 1.8 collective-permute-done.4
  240.7 202.8 %while.53 = (s32[]{:T(128)}, f32[8,16,512]{2,1,0:T(8,128)S(1)}, s32[8]{0:T(128)S(1)}, f32[16,6144]{1,0:T(8,128)S(1)}, f32[3,6144]{1,0:T(4,128)S(1)}, /*index=5*/...) while((s32[]{:T(128)}, f32[8,16,512]{2,1,0:T(8,128)S(1)}, ...), condition=%wide.region_3.4_spmd, body=%wide.region_2.3_spmd.sunk | while | flops 246620224 | bytes 1092197 | solution.py:60
  443.7 6.1 collective-permute-start.7
  450.1 1.5 collective-permute-done.6
  451.8 203.8 %while.54 = (s32[]{:T(128)}, f32[8,16,512]{2,1,0:T(8,128)S(1)}, s32[8]{0:T(128)S(1)}, f32[16,6144]{1,0:T(8,128)S(1)}, f32[3,6144]{1,0:T(4,128)S(1)}, /*index=5*/...) while((s32[]{:T(128)}, f32[8,16,512]{2,1,0:T(8,128)S(1)}, ...), condition=%wide.region_5.6_spmd, body=%wide.region_4.5_spmd.sunk | while | flops 246620224 | bytes 1092197 | solution.py:60
  656.7 5.3 collective-permute-start.9
  662.3 1.7 collective-permute-done.8
  664.1 207.7 %while.55 = (s32[]{:T(128)}, f32[8,16,512]{2,1,0:T(8,128)S(1)}, s32[8]{0:T(128)S(1)}, f32[16,6144]{1,0:T(8,128)S(1)}, f32[3,6144]{1,0:T(4,128)S(1)}, /*index=5*/...) while((s32[]{:T(128)}, f32[8,16,512]{2,1,0:T(8,128)S(1)}, ...), condition=%wide.region_7.8_spmd, body=%wide.region_6.7_spmd.sunk | while | flops 246620224 | bytes 1092197 | solution.py:60
  873.4 45.4 %all-gather.2.cloned.1.call-done = f32[5,32,4096]{2,1,0:T(8,128)} async-done(((f32[5,16,4096]{2,1,0:T(8,128)}), f32[5,32,4096]{2,1,0:T(8,128)}) %all-gather.2.cloned.1.call-update) | async-done | bytes 2621456 | tf_op jit(solution)/shard_map/all_gather | solution.py:119
  918.8 5.6 fusion.2577
  924.9 1.3 copy-done.1
  926.2 1.6 bitcast_add_fusion
  927.8 1111.1 %all-reduce.2.cloned.1.call-done = f32[160,160]{0,1:T(8,128)} async-done(((f32[160,160]{0,1:T(8,128)}), f32[160,160]{0,1:T(8,128)}) %all-reduce.2.cloned.1.call-update) | async-done | bytes 102416 | tf_op jit(solution)/shard_map/psum | solution.py:121
  2039.9 11.7 cholesky.44
  2053.0 9.8 custom-call.10
  2064.0 12.0 cholesky.55
  2077.3 9.8 custom-call.11
  2087.9 2.7 fusion.2532
  2093.9 2.0 copy.30
  (960 shorter events, 433.1 us)
Async XLA Ops:
  7.2 911.6 %all-gather.2.cloned.1.call-start = ((), (), s32[]{:S(2)}) async-start(), calls=%async_computation | async-start | bytes 3932160 | tf_op jit(solution)/shard_map/all_gather | solution.py:119
  8.1 18.1 collective-permute-start.2
  11.2 15.0 collective-permute-start.3
  17.7 8.5 collective-permute-start
  17.8 8.4 collective-permute-start.1
  26.3 206.0 %copy-start.3 = (f32[16,1,4096]{2,1,0:T(1,128)S(1)}, f32[16,1,4096]{2,1,0:T(1,128)}, u32[]{:S(2)}) copy-start(f32[16,1,4096]{2,1,0:T(1,128)} %param.13) | copy-start | bytes 786436
  232.5 8.2 collective-permute-start.4
  232.8 7.9 collective-permute-start.5
  443.6 8.0 collective-permute-start.6
  443.7 8.0 collective-permute-start.7
  655.7 8.3 collective-permute-start.8
  656.7 7.3 collective-permute-start.9
  872.0 1.1 copy-start.4
  873.1 1165.8 %all-reduce.2.cloned.1.call-start = ((), (), s32[]{:S(2)}) async-start(), calls=%async_computation.1 | async-start | bytes 327680 | tf_op jit(solution)/shard_map/psum | solution.py:121
  918.8 5.6 copy-start
  924.9 1.3 copy-start.1
  2063.9 27.7 %copy-start.2 = (f32[4,32,4096]{2,1,0:T(8,128)S(1)}, f32[4,32,4096]{2,1,0:T(8,128)}, u32[]{:S(2)}) copy-start(f32[4,32,4096]{2,1,0:T(8,128)} %copy-done.1) | copy-start | bytes 6291460
Sparse Core Ops, SparseCore 0:
  873.2 45.5 all-gather.1
  924.5 1114.2 all-reduce.1
where the time goes:
time: 2130 us; the launch traced here: 2100 us
  waiting for transfers between devices  1160 us (54%)
  loops' own time  407 us (19%)
  matrix products  296 us (14%)
  local copies, waits for them, and re-layouts  140 us (7%)
  other arithmetic  51.7 us (2%)
  starting transfers between devices  32.9 us (2%)
    psum x1, waiting for transfers between devices, local(): gram = lax.psum(row_products(flat), ('blk', 'leaf'))  1110 us
    another operation x4, loops' own time, band_product(): lax.scan(turn, jnp.zeros((), jnp.int32), jnp.arange(8, dtype=jnp.int32))  407 us
    dot_general x576, matrix products, turn(): total = total + jnp.dot(near_field, tile, precision=exact)  284 us
    dynamic_slice x160, local copies, waits for them, and re-layouts, turn(): listed = lax.dynamic_index_in_dim(weights[offset], block, 0, False)  105 us
    all_gather x1, waiting for transfers between devices, local(): whole = lax.all_gather(half_panel, 'rhs', axis=1, tiled=True)  45.4 us
  transfers between devices with their start and end apart: 12, of which 6 were waited for; matrix products, arithmetic and copies ran while one was open for 0% of the time, Pallas kernels for 0%

commit v1 on v0

--- a/solution.py
+++ b/solution.py
@@ -63,7 +63,7 @@
 
 def galerkin(gram, count_points, count_sides):
     normed = gram / count_points
-    basis_count = normed.shape[0] - count_sides
+    basis_count = normed.shape[0]
     gram_basis = normed[:basis_count, :basis_count]
     factor_low = jnp.linalg.cholesky(gram_basis)
     inverse_low = lax.linalg.triangular_solve(
@@ -84,8 +84,21 @@
     return (inverse_low, combo)
 
 
-def row_products(rows):
-    return lax.dot_general(rows, rows, (((1,), (1,)), ((), ())), precision=exact)
+def row_products(rows, cols):
+    return lax.dot_general(rows, cols, (((1,), (1,)), ((), ())), precision=exact)
+
+
+def butterfly_sum(x, axes):
+    for axis in axes:
+        count = lax.axis_size(axis)
+        if count & (count - 1):
+            x = lax.psum(x, axis)
+            continue
+        step = 1
+        while step < count:
+            x = x + lax.ppermute(x, axis, [(i, i ^ step) for i in range(count)])
+            step *= 2
+    return x
 
 
 def local(residual, points, noise, block_list):
@@ -118,7 +131,7 @@
     sides_here = field.shape[0]
     whole = lax.all_gather(half_panel, "rhs", axis=1, tiled=True)
     flat = whole.reshape(-1, own_rows)
-    gram = lax.psum(row_products(flat), ("blk", "leaf"))
+    gram = butterfly_sum(row_products(flat[: S * M], flat), ("leaf", "blk"))
     inverse_low, combo = galerkin(gram, count_points, M)
     first_rows = flat[: S * M]
     image = flat[M:] + centre_shift * first_rows

time: 2130 us -> 1060 us (0.50)
  waiting for transfers between devices: 1160 us -> 79.6 us
  loops' own time: 407 us -> 429 us
    psum x1 -> x0, waiting for transfers between devices: 1110 us -> none  [local(): gram = lax.psum(row_products(flat), ('blk', 'leaf'))]
    another operation x4, loops' own time: 407 us -> 429 us  [band_product(): lax.scan(turn, jnp.zeros((), jnp.int32), jnp.arange(8, dtype=jnp.int32))]
    ppermute x0 -> x7, waiting for transfers between devices: none -> 21.3 us  [butterfly_sum(): x = x + lax.ppermute(x, axis, [(i, i ^ step) for i in range(count)])]
  transfers between devices with their start and end apart: 12 -> 18, of which waited for: 6 -> 14; matrix products, arithmetic and copies ran while one was open for 0% -> 1% of each run, Pallas kernels for 0% -> 0%
where the time goes in v1:
time: 1060 us; the launch traced here: 1040 us
  loops' own time  429 us (40%)
  matrix products  279 us (26%)
  local copies, waits for them, and re-layouts  147 us (14%)
  waiting for transfers between devices  79.6 us (8%)
  other arithmetic  52.4 us (5%)
  starting transfers between devices  40.6 us (4%)
  between operations  15 us (1%)
    another operation x4, loops' own time, band_product(): lax.scan(turn, jnp.zeros((), jnp.int32), jnp.arange(8, dtype=jnp.int32))  429 us
    dot_general x576, matrix products, turn(): total = total + jnp.dot(near_field, tile, precision=exact)  272 us
    dynamic_slice x160, local copies, waits for them, and re-layouts, turn(): listed = lax.dynamic_index_in_dim(weights[offset], block, 0, False)  109 us
    all_gather x1, waiting for transfers between devices, local(): whole = lax.all_gather(half_panel, 'rhs', axis=1, tiled=True)  39.6 us
    ppermute x7, waiting for transfers between devices, butterfly_sum(): x = x + lax.ppermute(x, axis, [(i, i ^ step) for i in range(count)])  21.3 us
  transfers between devices with their start and end apart: 18, of which 14 were waited for; matrix products, arithmetic and copies ran while one was open for 1% of the time, Pallas kernels for 0%

profile of v1, /device:TPU:16, one launch (start us, length us, event | category | flops | bytes accessed | tf_op | source)
XLA Modules:
  0.0 1043.4 jit_solution(11603520780824057718)
XLA Ops:
  8.3 8.4 collective-permute-start.1
  17.6 5.7 collective-permute-start.3
  26.0 4.6 collective-permute-done.2
  30.8 209.0 %while.52 = (s32[]{:T(128)}, f32[8,16,512]{2,1,0:T(8,128)S(1)}, s32[8]{0:T(128)S(1)}, f32[16,6144]{1,0:T(8,128)S(1)}, f32[3,6144]{1,0:T(4,128)S(1)}, /*index=5*/...) while((s32[]{:T(128)}, f32[8,16,512]{2,1,0:T(8,128)S(1)}, ...), condition=%wide.region_1.2_spmd, body=%wide.region_0.1_spmd.sunk | while | flops 246620224 | bytes 1092197 | solution.py:60
  246.3 3.1 collective-permute-done.4
  249.6 208.9 %while.53 = (s32[]{:T(128)}, f32[8,16,512]{2,1,0:T(8,128)S(1)}, s32[8]{0:T(128)S(1)}, f32[16,6144]{1,0:T(8,128)S(1)}, f32[3,6144]{1,0:T(4,128)S(1)}, /*index=5*/...) while((s32[]{:T(128)}, f32[8,16,512]{2,1,0:T(8,128)S(1)}, ...), condition=%wide.region_3.4_spmd, body=%wide.region_2.3_spmd.sunk | while | flops 246620224 | bytes 1092197 | solution.py:60
  458.9 3.9 collective-permute-start.6
  467.3 208.6 %while.54 = (s32[]{:T(128)}, f32[8,16,512]{2,1,0:T(8,128)S(1)}, s32[8]{0:T(128)S(1)}, f32[16,6144]{1,0:T(8,128)S(1)}, f32[3,6144]{1,0:T(4,128)S(1)}, /*index=5*/...) while((s32[]{:T(128)}, f32[8,16,512]{2,1,0:T(8,128)S(1)}, ...), condition=%wide.region_5.6_spmd, body=%wide.region_4.5_spmd.sunk | while | flops 246620224 | bytes 1092197 | solution.py:60
  676.3 3.7 collective-permute-start.8
  684.5 209.2 %while.55 = (s32[]{:T(128)}, f32[8,16,512]{2,1,0:T(8,128)S(1)}, s32[8]{0:T(128)S(1)}, f32[16,6144]{1,0:T(8,128)S(1)}, f32[3,6144]{1,0:T(4,128)S(1)}, /*index=5*/...) while((s32[]{:T(128)}, f32[8,16,512]{2,1,0:T(8,128)S(1)}, ...), condition=%wide.region_7.8_spmd, body=%wide.region_6.7_spmd.sunk | while | flops 246620224 | bytes 1092197 | solution.py:60
  895.1 39.6 %all-gather.2.cloned.1.call-done = f32[5,32,4096]{2,1,0:T(8,128)} async-done(((f32[5,16,4096]{2,1,0:T(8,128)}), f32[5,32,4096]{2,1,0:T(8,128)}) %all-gather.2.cloned.1.call-update) | async-done | bytes 2621456 | tf_op jit(solution)/shard_map/all_gather | solution.py:132
  934.7 4.1 fusion.2570
  943.7 3.3 collective-permute-done.11
  947.6 5.4 collective-permute-done.12
  953.1 3.0 collective-permute-start.13
  956.1 3.3 collective-permute-done.13
  961.0 3.8 collective-permute-done.14
  966.7 4.3 collective-permute-done.15
  971.1 6.3 collective-permute-start.16
  977.4 3.2 bitcast_add_fusion
  980.7 11.7 %cholesky.44 = f32[128,128]{1,0:T(8,128)S(1)} custom-call(f32[128,128]{1,0:T(8,128)S(1)} %fusion.2546), custom_call_target="Cholesky" | custom-call | tf_op jit(solution)/shard_map/jit(cholesky)/cholesky | solution.py:68
  993.8 9.8 custom-call.10
  1004.8 11.7 %cholesky.55 = f32[128,128]{1,0:T(8,128)S(1)} custom-call(f32[128,128]{1,0:T(8,128)S(1)} %fusion.2542), custom_call_target="Cholesky" | custom-call | tf_op jit(solution)/shard_map/jit(cholesky)/cholesky | solution.py:78
  1017.9 10.0 custom-call.11
  (975 shorter events, 450.1 us)
Async XLA Ops:
  7.2 927.6 %all-gather.2.cloned.1.call-start = ((), (), s32[]{:S(2)}) async-start(), calls=%async_computation | async-start | bytes 3932160 | tf_op jit(solution)/shard_map/all_gather | solution.py:132
  8.3 22.3 %collective-permute-start.1 = (f32[16,1024]{1,0:T(8,128)S(1)}, f32[16,1024]{1,0:T(8,128)S(1)}, u32[]{:S(2)}, u32[]{:S(2)}) collective-permute-start(f32[16,1024]{1,0:T(8,128)S(1)} %get-tuple-element.897), channel_id=1, source_target_pairs={{16,0},{32,16},{48,32},{64,48},{80,64},{96,80},{112,96},{128,112},... | collective-permute-start | bytes 196616 | tf_op jit(solution)/shard_map/ppermute | solution.py:26
  16.7 14.0 %collective-permute-start = (f32[16,1024]{1,0:T(8,128)S(1)}, f32[16,1024]{1,0:T(8,128)S(1)}, u32[]{:S(2)}, u32[]{:S(2)}) collective-permute-start(f32[16,1024]{1,0:T(8,128)S(1)} %get-tuple-element.896), channel_id=1, source_target_pairs={{0,16},{16,32},{32,48},{48,64},{64,80},{80,96},{96,112},{112,128},... | collective-permute-start | bytes 196616 | tf_op jit(solution)/shard_map/ppermute | solution.py:25
  17.6 8.5 collective-permute-start.3
  23.3 7.4 collective-permute-start.2
  30.8 209.3 %copy-start.2 = (f32[16,1,4096]{2,1,0:T(1,128)S(1)}, f32[16,1,4096]{2,1,0:T(1,128)}, u32[]{:S(2)}) copy-start(f32[16,1,4096]{2,1,0:T(1,128)} %param.13) | copy-start | bytes 786436
  240.3 6.1 collective-permute-start.5
  241.6 7.9 collective-permute-start.4
  458.8 5.8 collective-permute-start.7
  458.9 8.4 collective-permute-start.6
  676.2 5.8 collective-permute-start.9
  676.3 8.1 collective-permute-start.8
  894.1 1.1 copy-start.3
  934.7 4.1 copy-start
  941.0 1.4 collective-permute-start.10
  942.4 4.6 collective-permute-start.11
  947.0 6.0 collective-permute-start.12
  953.1 6.2 collective-permute-start.13
  959.3 5.4 collective-permute-start.14
  964.8 6.3 collective-permute-start.15
  971.1 9.5 collective-permute-start.16
  1027.9 2.8 copy-start.1
Sparse Core Ops, SparseCore 0:
  895.3 39.4 all-gather.1

commit v2 on v1

--- a/solution.py
+++ b/solution.py
@@ -37,28 +37,22 @@
     return remain * remain * (remain * remain) * (4.0 * radius + 1.0) * (amplitude / SUPPORT)
 
 
-def band_product(field_wide, points_wide, weights, rows_out):
-    per_turn = rows_out // 8
+def band_tiles(points_wide, weights, rows_out):
+    width = 2 * REACH + 1
+    blocks = points_wide.reshape(3, -1, BS)
+    own = blocks[:, REACH : REACH + rows_out]
+    near = jnp.stack([blocks[:, k : k + rows_out] for k in range(width)], axis=2)
+    tiles = jax.vmap(jax.vmap(kernel_tile, in_axes=(1, None)), in_axes=(1, 1))(near, own)
+    return tiles * jnp.transpose(weights)[:, :, None, None]
+
+
+def band_product(field_wide, tiles, rows_out):
+    width = 2 * REACH + 1
     count = field_wide.shape[0]
-
-    def turn(carry, index):
-        pieces = []
-        for inner in range(per_turn):
-            block = index * per_turn + inner
-            own_points = lax.dynamic_slice_in_dim(points_wide, (block + REACH) * BS, BS, 1)
-            total = jnp.zeros((count, BS), jnp.float32)
-            for offset in range(2 * REACH + 1):
-                column_at = (block + offset) * BS
-                near_points = lax.dynamic_slice_in_dim(points_wide, column_at, BS, 1)
-                near_field = lax.dynamic_slice_in_dim(field_wide, column_at, BS, 1)
-                listed = lax.dynamic_index_in_dim(weights[offset], block, 0, False)
-                tile = kernel_tile(near_points, own_points) * listed
-                total = total + jnp.dot(near_field, tile, precision=exact)
-            pieces.append(total)
-        return (carry, jnp.concatenate(pieces, axis=1))
-
-    carry, parts = lax.scan(turn, jnp.zeros((), jnp.int32), jnp.arange(8, dtype=jnp.int32))
-    return jnp.moveaxis(parts, 0, 1).reshape(count, rows_out * BS)
+    blocks = field_wide.reshape(count, -1, BS)
+    near = jnp.stack([blocks[:, k : k + rows_out] for k in range(width)], axis=2)
+    out = jnp.einsum("mbkq,bkqp->mbp", near, tiles, precision=exact)
+    return out.reshape(count, rows_out * BS)
 
 
 def galerkin(gram, count_points, count_sides):
@@ -118,11 +112,12 @@
     rim = REACH * BS
     coords_wide = extended(coords, (("blk", 1),), rim)
     own_weights = lax.dynamic_slice_in_dim(wrapped, first_block + margin, own_blocks, 1)
+    tiles = lax.optimization_barrier(band_tiles(coords_wide, own_weights, own_blocks))
     current = field
     for power_step in range(S):
         widened = extended(current, (("blk", 1),), rim)
         current = (
-            band_product(widened, coords_wide, own_weights, own_blocks)
+            band_product(widened, tiles, own_blocks)
             + (nugget - centre_shift) * current
         )
         powers.append(current)

time: 1060 us -> 350 us (0.33); the launches traced: 1040 us -> 347 us
  loops' own time: 429 us -> 0 us
  matrix products: 279 us -> 103 us
  local copies, waits for them, and re-layouts: 147 us -> 21.2 us
  other arithmetic: 52.4 us -> 86.9 us
    another operation x4 -> x0, loops' own time: 429 us -> none  [band_product(): lax.scan(turn, jnp.zeros((), jnp.int32), jnp.arange(8, dtype=jnp.int32))]
    dot_general x576 -> x4, matrix products: 272 us -> 95.8 us  [band_product(): out = jnp.einsum('mbkq,bkqp->mbp', near, tiles, precision=exact)]
    dynamic_slice x192 -> x0, local copies, waits for them, and re-layouts: 128 us -> none  [the longest x160 109 us: turn(): listed = lax.dynamic_index_in_dim(weights[offset], block, 0, False)]
    mul x0 -> x2, other arithmetic: none -> 35.5 us  [band_tiles(): return tiles * jnp.transpose(weights)[:, :, None, None]]
    ppermute x5, starting transfers between devices: 15.6 us -> 29.7 us  [extended(): after = lax.ppermute(leading, axis, down)]
  transfers between devices with their start and end apart: 18 -> 18, of which waited for: 14 -> 11; matrix products, arithmetic and copies ran while one was open for 1% -> 13% of each run, Pallas kernels for 0% -> 0%
where the time goes in v2:
time: 350 us; the launch traced here: 347 us
  matrix products  103 us (29%)
  other arithmetic  86.9 us (25%)
  waiting for transfers between devices  72 us (21%)
  starting transfers between devices  48.1 us (14%)
  local copies, waits for them, and re-layouts  21.2 us (6%)
  between operations  15.3 us (4%)
    dot_general x4, matrix products, band_product(): out = jnp.einsum('mbkq,bkqp->mbp', near, tiles, precision=exact)  95.8 us
    all_gather x1, waiting for transfers between devices, local(): whole = lax.all_gather(half_panel, 'rhs', axis=1, tiled=True)  45.7 us
    mul x2, other arithmetic, band_tiles(): return tiles * jnp.transpose(weights)[:, :, None, None]  35.5 us
    ppermute x5, starting transfers between devices, extended(): after = lax.ppermute(leading, axis, down)  29.7 us
    ppermute x7, waiting for transfers between devices, butterfly_sum(): x = x + lax.ppermute(x, axis, [(i, i ^ step) for i in range(count)])  21.4 us
    ppermute x7, starting transfers between devices, butterfly_sum(): x = x + lax.ppermute(x, axis, [(i, i ^ step) for i in range(count)])  14.9 us
    unnamed x59, local copies, waits for them, and re-layouts  13.7 us
    another operation x3, other arithmetic, galerkin(): proj_factor = jnp.linalg.cholesky(projected)  12.6 us
  transfers between devices with their start and end apart: 18, of which 11 were waited for; matrix products, arithmetic and copies ran while one was open for 13% of the time, Pallas kernels for 0%

profile of v2, /device:TPU:16, one launch (start us, length us, event | category | flops | bytes accessed | tf_op | source)
XLA Modules:
  0.0 346.6 jit_solution(17258190451148754818)
XLA Ops:
  8.1 3.1 collective-permute-start
  11.2 5.4 %collective-permute-start.1 = (f32[3,1024]{1,0:T(4,128)S(1)}, f32[3,1024]{1,0:T(4,128)S(1)}, u32[]{:S(2)}, u32[]{:S(2)}) collective-permute-start(f32[3,1024]{1,0:T(4,128)S(1)} %get-tuple-element.65), channel_id=1, source_target_pairs={{16,0},{32,16},{48,32},{64,48},{80,64},{96,80},{112,96},{128,112},... | collective-permute-start | bytes 36872 | tf_op jit(solution)/shard_map/ppermute | solution.py:26
  17.8 5.8 %collective-permute-start.3 = (f32[16,1024]{1,0:T(8,128)S(1)}, f32[16,1024]{1,0:T(8,128)S(1)}, u32[]{:S(2)}, u32[]{:S(2)}) collective-permute-start(f32[16,1024]{1,0:T(8,128)S(1)} %get-tuple-element.60), channel_id=1, source_target_pairs={{16,0},{32,16},{48,32},{64,48},{80,64},{96,80},{112,96},{128,112},... | collective-permute-start | bytes 196616 | tf_op jit(solution)/shard_map/ppermute | solution.py:26
  27.0 35.4 %multiply_multiply_fusion = f32[16,9,256,256]{3,2,1,0:T(8,128)} fusion(f32[16,9]{1,0:T(8,128)S(1)} %copy.52, f32[16,256]{1,0:T(8,128)S(1)} %get-tuple-element.62, f32[16,9,256]{2,1,0:T(8,128)S(1)} %copy.51, f32[16,256]{1,0:T(8,128)S(1)} %get-tuple-element.63, f32[16,9,256]{2,1,0:T(8,128)S(1)} %copy.50, f32[16,256]{1,0:T(8,128)S(1)} %get-tuple-element.61, ...), kind=kLoop, calls=%fused_computation | loop fusion | flops 160432128 | bytes 38240832 | tf_op jit(solution)/shard_map/mul | solution.py:46
  64.3 24.0 %fusion.82 = f32[16,256,16,1]{1,2,3,0:T(8,128)S(1)} fusion(f32[16,9,256,256]{3,2,1,0:T(8,128)} %multiply_multiply_fusion, f32[16,16,9,256]{3,0,2,1:T(8,128)S(1)} %fusion.28), kind=kOutput, calls=%fused_computation.187 | convolution fusion | flops 1811939328 | bytes 40370176 | tf_op jit(solution)/shard_map/mbkq,bkqp->mbp/dot_general | solution.py:54
  88.6 5.9 %collective-permute-start.5 = (f32[16,1024]{1,0:T(8,128)S(1)}, f32[16,1024]{1,0:T(8,128)S(1)}, u32[]{:S(2)}, u32[]{:S(2)}) collective-permute-start(f32[16,1024]{1,0:T(8,128)S(1)} %get-tuple-element.58), channel_id=1, source_target_pairs={{16,0},{32,16},{48,32},{64,48},{80,64},{96,80},{112,96},{128,112},... | collective-permute-start | bytes 196616 | tf_op jit(solution)/shard_map/ppermute | solution.py:26
  98.3 23.9 %fusion.83 = f32[16,256,16,1]{1,2,3,0:T(8,128)S(1)} fusion(f32[16,9,256,256]{3,2,1,0:T(8,128)} %multiply_multiply_fusion, f32[16,16,9,256]{3,0,2,1:T(8,128)S(1)} %fusion.19), kind=kOutput, calls=%fused_computation.188 | convolution fusion | flops 1811939328 | bytes 40370176 | tf_op jit(solution)/shard_map/mbkq,bkqp->mbp/dot_general | solution.py:54
  122.4 6.4 %collective-permute-start.7 = (f32[16,1024]{1,0:T(8,128)S(1)}, f32[16,1024]{1,0:T(8,128)S(1)}, u32[]{:S(2)}, u32[]{:S(2)}) collective-permute-start(f32[16,1024]{1,0:T(8,128)S(1)} %get-tuple-element.56), channel_id=1, source_target_pairs={{16,0},{32,16},{48,32},{64,48},{80,64},{96,80},{112,96},{128,112},... | collective-permute-start | bytes 196616 | tf_op jit(solution)/shard_map/ppermute | solution.py:26
  132.7 23.9 %fusion.84 = f32[16,256,16,1]{1,2,3,0:T(8,128)S(1)} fusion(f32[16,9,256,256]{3,2,1,0:T(8,128)} %multiply_multiply_fusion, f32[16,16,9,256]{3,0,2,1:T(8,128)S(1)} %fusion.10), kind=kOutput, calls=%fused_computation.189 | convolution fusion | flops 1811939328 | bytes 40370176 | tf_op jit(solution)/shard_map/mbkq,bkqp->mbp/dot_general | solution.py:54
  156.8 6.2 %collective-permute-start.9 = (f32[16,1024]{1,0:T(8,128)S(1)}, f32[16,1024]{1,0:T(8,128)S(1)}, u32[]{:S(2)}, u32[]{:S(2)}) collective-permute-start(f32[16,1024]{1,0:T(8,128)S(1)} %get-tuple-element.54), channel_id=1, source_target_pairs={{16,0},{32,16},{48,32},{64,48},{80,64},{96,80},{112,96},{128,112},... | collective-permute-start | bytes 196616 | tf_op jit(solution)/shard_map/ppermute | solution.py:26
  166.9 23.9 %convolution_bitcast_fusion.2 = f32[16,16,256]{2,0,1:T(8,128)S(1)} fusion(f32[16,9,256,256]{3,2,1,0:T(8,128)} %multiply_multiply_fusion, f32[16,16,9,256]{3,0,2,1:T(8,128)S(1)} %fusion.1), kind=kOutput, calls=%fused_computation.6 | convolution fusion | flops 1811939328 | bytes 40370176 | tf_op jit(solution)/shard_map/mbkq,bkqp->mbp/dot_general | solution.py:54
  192.2 45.7 %all-gather.2.cloned.1.call-done = f32[5,32,4096]{2,1,0:T(8,128)} async-done(((f32[5,16,4096]{2,1,0:T(8,128)}), f32[5,32,4096]{2,1,0:T(8,128)}) %all-gather.2.cloned.1.call-update) | async-done | bytes 2621456 | tf_op jit(solution)/shard_map/all_gather | solution.py:127
  237.9 4.1 %fusion.71 = (f32[4,32,4096]{2,1,0:T(8,128)}, f32[4,32,4096]{2,1,0:T(8,128)S(1)}) fusion(f32[5,32,4096]{2,1,0:T(8,128)} %all-gather.2.cloned.1.call-done), kind=kLoop, calls=%fused_computation.176 | loop fusion | bytes 8388608 | tf_op jit(solution)/shard_map/slice | solution.py:132
  246.9 3.3 collective-permute-done.11
  250.8 5.4 %collective-permute-done.12 = f32[128,160]{0,1:T(8,128)S(1)} collective-permute-done((f32[128,160]{0,1:T(8,128)S(1)}, f32[128,160]{0,1:T(8,128)S(1)}, u32[]{:S(2)}, u32[]{:S(2)}) %collective-permute-start.12) | collective-permute-done | bytes 81952 | tf_op jit(solution)/shard_map/ppermute | solution.py:93
  259.2 3.3 collective-permute-done.13
  264.2 3.8 %collective-permute-done.14 = f32[128,160]{0,1:T(8,128)S(1)} collective-permute-done((f32[128,160]{0,1:T(8,128)S(1)}, f32[128,160]{0,1:T(8,128)S(1)}, u32[]{:S(2)}, u32[]{:S(2)}) %collective-permute-start.14) | collective-permute-done | bytes 81952 | tf_op jit(solution)/shard_map/ppermute | solution.py:93
  269.9 4.3 %collective-permute-done.15 = f32[128,160]{0,1:T(8,128)S(1)} collective-permute-done((f32[128,160]{0,1:T(8,128)S(1)}, f32[128,160]{0,1:T(8,128)S(1)}, u32[]{:S(2)}, u32[]{:S(2)}) %collective-permute-start.15) | collective-permute-done | bytes 81952 | tf_op jit(solution)/shard_map/ppermute | solution.py:93
  274.3 6.3 %collective-permute-start.16 = (f32[128,160]{0,1:T(8,128)S(1)}, f32[128,160]{0,1:T(8,128)S(1)}, u32[]{:S(2)}, u32[]{:S(2)}) collective-permute-start(f32[128,160]{0,1:T(8,128)S(1)} %add.155), channel_id=1, source_target_pairs={{0,128},{16,144},{32,160},{48,176},{64,192},{80,208},{96,224},{112... | collective-permute-start | bytes 245768 | tf_op jit(solution)/shard_map/ppermute | solution.py:93
  280.6 3.2 bitcast_add_fusion
  283.9 11.7 %cholesky.44 = f32[128,128]{1,0:T(8,128)S(1)} custom-call(f32[128,128]{1,0:T(8,128)S(1)} %fusion.49), custom_call_target="Cholesky" | custom-call | tf_op jit(solution)/shard_map/jit(cholesky)/cholesky | solution.py:62
  297.0 9.8 %custom-call.10 = f32[1,128,128]{1,2,0:T(8,128)S(1)} custom-call(f32[1,128,128]{2,1,0:T(8,128)S(1)} %fusion.38), custom_call_target="InvertDiagBlocksLowerTriangular" | custom-call | tf_op jit(solution)/shard_map/triangular_solve | solution.py:63
  311.3 11.9 %cholesky.55 = f32[128,128]{1,0:T(8,128)S(1)} custom-call(f32[128,128]{1,0:T(8,128)S(1)} %fusion.45), custom_call_target="Cholesky" | custom-call | tf_op jit(solution)/shard_map/jit(cholesky)/cholesky | solution.py:72
  324.6 9.8 %custom-call.11 = f32[1,128,128]{1,2,0:T(8,128)S(1)} custom-call(f32[1,128,128]{2,1,0:T(8,128)S(1)} %fusion.39), custom_call_target="InvertDiagBlocksLowerTriangular" | custom-call | tf_op jit(solution)/shard_map/triangular_solve | solution.py:74
  (164 shorter events, 44.7 us)
Async XLA Ops:
  7.2 230.7 %all-gather.2.cloned.1.call-start = ((), (), s32[]{:S(2)}) async-start(), calls=%async_computation | async-start | bytes 3932160 | tf_op jit(solution)/shard_map/all_gather | solution.py:127
  8.1 18.3 %collective-permute-start = (f32[3,1024]{1,0:T(4,128)S(1)}, f32[3,1024]{1,0:T(4,128)S(1)}, u32[]{:S(2)}, u32[]{:S(2)}) collective-permute-start(f32[3,1024]{1,0:T(4,128)S(1)} %get-tuple-element.64), channel_id=1, source_target_pairs={{0,16},{16,32},{32,48},{48,64},{64,80},{80,96},{96,112},{112,128},... | collective-permute-start | bytes 36872 | tf_op jit(solution)/shard_map/ppermute | solution.py:25
  11.2 15.2 %collective-permute-start.1 = (f32[3,1024]{1,0:T(4,128)S(1)}, f32[3,1024]{1,0:T(4,128)S(1)}, u32[]{:S(2)}, u32[]{:S(2)}) collective-permute-start(f32[3,1024]{1,0:T(4,128)S(1)} %get-tuple-element.65), channel_id=1, source_target_pairs={{16,0},{32,16},{48,32},{64,48},{80,64},{96,80},{112,96},{128,112},... | collective-permute-start | bytes 36872 | tf_op jit(solution)/shard_map/ppermute | solution.py:26
  17.7 44.7 %collective-permute-start.2 = (f32[16,1024]{1,0:T(8,128)S(1)}, f32[16,1024]{1,0:T(8,128)S(1)}, u32[]{:S(2)}, u32[]{:S(2)}) collective-permute-start(f32[16,1024]{1,0:T(8,128)S(1)} %get-tuple-element.59), channel_id=1, source_target_pairs={{0,16},{16,32},{32,48},{48,64},{64,80},{80,96},{96,112},{112,128},... | collective-permute-start | bytes 196616 | tf_op jit(solution)/shard_map/ppermute | solution.py:25
  17.8 44.6 %collective-permute-start.3 = (f32[16,1024]{1,0:T(8,128)S(1)}, f32[16,1024]{1,0:T(8,128)S(1)}, u32[]{:S(2)}, u32[]{:S(2)}) collective-permute-start(f32[16,1024]{1,0:T(8,128)S(1)} %get-tuple-element.60), channel_id=1, source_target_pairs={{16,0},{32,16},{48,32},{64,48},{80,64},{96,80},{112,96},{128,112},... | collective-permute-start | bytes 196616 | tf_op jit(solution)/shard_map/ppermute | solution.py:26
  64.3 24.0 %copy-start.2 = (f32[16,1,4096]{2,1,0:T(1,128)S(1)}, f32[16,1,4096]{2,1,0:T(1,128)}, u32[]{:S(2)}) copy-start(f32[16,1,4096]{2,1,0:T(1,128)} %param.5) | copy-start | bytes 786436
  88.5 8.0 %collective-permute-start.4 = (f32[16,1024]{1,0:T(8,128)S(1)}, f32[16,1024]{1,0:T(8,128)S(1)}, u32[]{:S(2)}, u32[]{:S(2)}) collective-permute-start(f32[16,1024]{1,0:T(8,128)S(1)} %get-tuple-element.57), channel_id=1, source_target_pairs={{0,16},{16,32},{32,48},{48,64},{64,80},{80,96},{96,112},{112,128},... | collective-permute-start | bytes 196616 | tf_op jit(solution)/shard_map/ppermute | solution.py:25
  88.6 7.9 %collective-permute-start.5 = (f32[16,1024]{1,0:T(8,128)S(1)}, f32[16,1024]{1,0:T(8,128)S(1)}, u32[]{:S(2)}, u32[]{:S(2)}) collective-permute-start(f32[16,1024]{1,0:T(8,128)S(1)} %get-tuple-element.58), channel_id=1, source_target_pairs={{16,0},{32,16},{48,32},{64,48},{80,64},{96,80},{112,96},{128,112},... | collective-permute-start | bytes 196616 | tf_op jit(solution)/shard_map/ppermute | solution.py:26
  122.4 8.2 %collective-permute-start.6 = (f32[16,1024]{1,0:T(8,128)S(1)}, f32[16,1024]{1,0:T(8,128)S(1)}, u32[]{:S(2)}, u32[]{:S(2)}) collective-permute-start(f32[16,1024]{1,0:T(8,128)S(1)} %get-tuple-element.55), channel_id=1, source_target_pairs={{0,16},{16,32},{32,48},{48,64},{64,80},{80,96},{96,112},{112,128},... | collective-permute-start | bytes 196616 | tf_op jit(solution)/shard_map/ppermute | solution.py:25
  122.4 8.3 %collective-permute-start.7 = (f32[16,1024]{1,0:T(8,128)S(1)}, f32[16,1024]{1,0:T(8,128)S(1)}, u32[]{:S(2)}, u32[]{:S(2)}) collective-permute-start(f32[16,1024]{1,0:T(8,128)S(1)} %get-tuple-element.56), channel_id=1, source_target_pairs={{16,0},{32,16},{48,32},{64,48},{80,64},{96,80},{112,96},{128,112},... | collective-permute-start | bytes 196616 | tf_op jit(solution)/shard_map/ppermute | solution.py:26
  156.7 8.3 %collective-permute-start.8 = (f32[16,1024]{1,0:T(8,128)S(1)}, f32[16,1024]{1,0:T(8,128)S(1)}, u32[]{:S(2)}, u32[]{:S(2)}) collective-permute-start(f32[16,1024]{1,0:T(8,128)S(1)} %get-tuple-element.53), channel_id=1, source_target_pairs={{0,16},{16,32},{32,48},{48,64},{64,80},{80,96},{96,112},{112,128},... | collective-permute-start | bytes 196616 | tf_op jit(solution)/shard_map/ppermute | solution.py:25
  156.8 8.2 %collective-permute-start.9 = (f32[16,1024]{1,0:T(8,128)S(1)}, f32[16,1024]{1,0:T(8,128)S(1)}, u32[]{:S(2)}, u32[]{:S(2)}) collective-permute-start(f32[16,1024]{1,0:T(8,128)S(1)} %get-tuple-element.54), channel_id=1, source_target_pairs={{16,0},{32,16},{48,32},{64,48},{80,64},{96,80},{112,96},{128,112},... | collective-permute-start | bytes 196616 | tf_op jit(solution)/shard_map/ppermute | solution.py:26
  191.1 1.1 copy-start.3
  237.9 4.1 %copy-start = (f32[5,32,4096]{2,1,0:T(8,128)S(1)}, f32[5,32,4096]{2,1,0:T(8,128)}, u32[]{:S(2)}) copy-start(f32[5,32,4096]{2,1,0:T(8,128)} %all-gather.2.cloned.1.call-done) | copy-start | bytes 7864324
  244.2 1.4 collective-permute-start.10
  245.6 4.6 %collective-permute-start.11 = (f32[128,160]{0,1:T(8,128)S(1)}, f32[128,160]{0,1:T(8,128)S(1)}, u32[]{:S(2)}, u32[]{:S(2)}) collective-permute-start(f32[128,160]{0,1:T(8,128)S(1)} %add.150), channel_id=1, source_target_pairs={{0,4},{2,6},{4,0},{6,2},{8,12},{10,14},{12,8},{14,10},{1,5},{3,7},... | collective-permute-start | bytes 245768 | tf_op jit(solution)/shard_map/ppermute | solution.py:93
  250.2 6.0 %collective-permute-start.12 = (f32[128,160]{0,1:T(8,128)S(1)}, f32[128,160]{0,1:T(8,128)S(1)}, u32[]{:S(2)}, u32[]{:S(2)}) collective-permute-start(f32[128,160]{0,1:T(8,128)S(1)} %add.151), channel_id=1, source_target_pairs={{0,8},{2,10},{4,12},{6,14},{8,0},{10,2},{12,4},{14,6},{1,9},{3,11}... | collective-permute-start | bytes 245768 | tf_op jit(solution)/shard_map/ppermute | solution.py:93
  256.3 6.2 %collective-permute-start.13 = (f32[128,160]{0,1:T(8,128)S(1)}, f32[128,160]{0,1:T(8,128)S(1)}, u32[]{:S(2)}, u32[]{:S(2)}) collective-permute-start(f32[128,160]{0,1:T(8,128)S(1)} %add.152), channel_id=1, source_target_pairs={{0,16},{16,0},{32,48},{48,32},{64,80},{80,64},{96,112},{112,96},{1... | collective-permute-start | bytes 245768 | tf_op jit(solution)/shard_map/ppermute | solution.py:93
  262.5 5.4 %collective-permute-start.14 = (f32[128,160]{0,1:T(8,128)S(1)}, f32[128,160]{0,1:T(8,128)S(1)}, u32[]{:S(2)}, u32[]{:S(2)}) collective-permute-start(f32[128,160]{0,1:T(8,128)S(1)} %add.153), channel_id=1, source_target_pairs={{0,32},{16,48},{32,0},{48,16},{64,96},{80,112},{96,64},{112,80},{1... | collective-permute-start | bytes 245768 | tf_op jit(solution)/shard_map/ppermute | solution.py:93
  267.9 6.3 %collective-permute-start.15 = (f32[128,160]{0,1:T(8,128)S(1)}, f32[128,160]{0,1:T(8,128)S(1)}, u32[]{:S(2)}, u32[]{:S(2)}) collective-permute-start(f32[128,160]{0,1:T(8,128)S(1)} %add.154), channel_id=1, source_target_pairs={{0,64},{16,80},{32,96},{48,112},{64,0},{80,16},{96,32},{112,48},{1... | collective-permute-start | bytes 245768 | tf_op jit(solution)/shard_map/ppermute | solution.py:93
  274.3 9.5 %collective-permute-start.16 = (f32[128,160]{0,1:T(8,128)S(1)}, f32[128,160]{0,1:T(8,128)S(1)}, u32[]{:S(2)}, u32[]{:S(2)}) collective-permute-start(f32[128,160]{0,1:T(8,128)S(1)} %add.155), channel_id=1, source_target_pairs={{0,128},{16,144},{32,160},{48,176},{64,192},{80,208},{96,224},{112... | collective-permute-start | bytes 245768 | tf_op jit(solution)/shard_map/ppermute | solution.py:93
  334.4 1.9 copy-start.1
Sparse Core Ops, SparseCore 0:
  192.4 45.5 all-gather.1
